TPU v7x, 32 devices: a whole 2x2x4 slice. The times are simulated.
32 devices in a mesh: dp: 2 (over y), seq: 16 (over z, x, core).
Axes of the slice: x: 2, y: 2, z: 4, core: 2. Of those that a mesh axis runs over, the one named last changes fastest.
Arguments:
- tokens: bfloat16 [2, 8192, 1024], P('dp', 'seq'), may hold values from -50 to 50
- w_query: bfloat16 [1024, 1024], P(None, 'dp'), may hold values from -0.1875 to 0.1875
- w_key: bfloat16 [1024, 1024], P(None, 'dp'), may hold values from -0.1875 to 0.1875
- w_value: bfloat16 [1024, 1024], P(None, 'dp'), may hold values from -0.1875 to 0.1875
- w_out: bfloat16 [1024, 1024], P('dp'), may hold values from -0.1875 to 0.1875
- norm_gain: float32 [1024], replicated, may hold values from 0.1 to 1.9
Outputs:
- layer_out: bfloat16 [2, 8192, 1024], P('dp', 'seq')
All inputs are finite; a program needn't handle non-finite values.
Results may differ from a plain program's by a relative error of at most 0.017.
Values may be sent and summed in bfloat16 or wider, within the bound.
A program may use at most 128 MiB of HBM per device.

v0:
```python
import jax
import jax.numpy as jnp
from jax import lax
from jax.sharding import PartitionSpec as P

H = 8
DH = 128


def entering(value, axis, join, neutral):
    place = lax.axis_index(axis)
    gathered = lax.all_gather(value.astype(jnp.bfloat16), axis)
    state = jnp.zeros_like(value) + jnp.asarray(neutral, value.dtype)

    def one(lap, state):
        return join(state, lax.dynamic_index_in_dim(gathered, lap, 0, False).astype(value.dtype))

    return lax.fori_loop(0, place, one, state)


def inner_block(query_heads, key_heads, value_heads):
    length = query_heads.shape[1]
    block = min(length, 512)
    scores = jnp.einsum("hid,hjd->hij", query_heads, key_heads, preferred_element_type=jnp.float32)
    row_ids = jnp.arange(0, block)[:, None]
    col_ids = jnp.arange(block)[None, :]
    scores = jnp.where(col_ids <= row_ids, scores, 0.0).astype(jnp.bfloat16)
    pieces = jnp.einsum("hij,hje->hie", scores, value_heads, preferred_element_type=jnp.float32)
    return pieces


def add_states(earlier, later):
    return earlier + later


def key_value_state(key_heads, value_heads):
    return jnp.einsum("htd,hte->hde", key_heads, value_heads, preferred_element_type=jnp.float32)


def attend(query_heads, key_heads, value_heads, prior):
    within = inner_block(query_heads, key_heads, value_heads)
    carried = jnp.einsum(
        "htd,hde->hte", query_heads, prior.astype(jnp.bfloat16), preferred_element_type=jnp.float32
    )
    return within + carried


def body(tokens, w_query, w_key, w_value, w_out, norm_gain):
    rows = tokens[0]
    length = rows.shape[0]
    stacked = jnp.stack([w_query, w_key, w_value], axis=0)
    projected = jnp.einsum(
        "td,pdc->ptc",
        rows,
        lax.all_gather(stacked, "dp", axis=2, tiled=True),
        preferred_element_type=jnp.float32,
    ).astype(jnp.bfloat16)
    query = projected[0]
    key = projected[1]
    value = projected[2]
    query_heads = query.reshape(length, H, DH).transpose(1, 0, 2)
    key_heads = key.reshape(length, H, DH).transpose(1, 0, 2)
    value_heads = value.reshape(length, H, DH).transpose(1, 0, 2)
    local_state = key_value_state(key_heads, value_heads)
    empty_state = jnp.zeros((H, DH, DH), jnp.float32)
    prior = entering(local_state, "seq", add_states, empty_state)
    mixed_raw = attend(query_heads, key_heads, value_heads, prior)
    scale = lax.rsqrt(jnp.mean(mixed_raw * mixed_raw, axis=-1, keepdims=True) + 1e-05)
    normed = (mixed_raw * scale * norm_gain.reshape(H, 1, DH)).astype(jnp.bfloat16)
    normed = normed.transpose(1, 0, 2).reshape(length, H * DH)
    result = jnp.dot(
        normed, lax.all_gather(w_out, "dp", axis=0, tiled=True), preferred_element_type=jnp.float32
    )
    return result.astype(jnp.bfloat16)[None]


def solution(mesh):
    in_specs = (
        P("dp", "seq", None),
        P(None, "dp"),
        P(None, "dp"),
        P(None, "dp"),
        P("dp", None),
        P(),
    )
    out_specs = P("dp", "seq", None)
    return jax.shard_map(body, mesh=mesh, in_specs=in_specs, out_specs=out_specs, check_vma=False)
```

profile of v0, /device:TPU:0, one launch (start us, length us, event | category | flops | bytes accessed | tf_op | source)
XLA Modules:
  0.0 202.5 jit_solution(4533514288469171736)
XLA Ops:
  6.5 0.0 copy-start
  6.5 0.0 all-gather.5.cloned.1.call-start
  6.5 1.6 copy.13
  8.1 1.5 copy.14
  9.6 2.3 %copy.15 = bf16[1024,512]{0,1:T(8,128)(2,1)} copy(bf16[1024,512]{1,0:T(8,128)(2,1)} %param.11) | data formatting | bytes 2097152 | tf_op args[3]
  11.9 3.3 %pad_maximum_fusion = bf16[3,1024,512]{1,2,0:T(8,128)(2,1)} fusion(bf16[1,1024,512]{1,2,0:T(8,128)(2,1)} %bitcast.57, bf16[1,1024,512]{1,2,0:T(8,128)(2,1)S(1)} %bitcast.56, bf16[1,1024,512]{1,2,0:T(8,128)(2,1)S(1)} %bitcast.55), kind=kLoop, calls=%fused_computation.6 | loop fusion | flops 3145728 | bytes 6291456 | tf_op jit(solution)/shard_map/stack | solution.py:51
  15.2 0.0 all-gather.5.cloned.1.call-update
  15.2 0.0 all-gather.9.cloned.1.call-start
  15.2 83.2 %all-gather.5.cloned.1.call-done = bf16[3,1024,1024]{1,2,0:T(8,128)(2,1)} async-done(((bf16[3,1024,512]{1,2,0:T(8,128)(2,1)}), bf16[3,1024,1024]{1,2,0:T(8,128)(2,1)}) %all-gather.5.cloned.1.call-update) | async-done | bytes 6291472 | tf_op jit(solution)/shard_map/all_gather | solution.py:55
  98.4 0.0 copy-done
  98.4 6.5 %convert_bitcast_fusion = bf16[3,512,1024]{1,2,0:T(8,128)(2,1)S(1)} fusion(bf16[3,1024,1024]{1,2,0:T(8,128)(2,1)} %all-gather.5.cloned.1.call-done, bf16[1,512,1024]{2,1,0:T(8,128)(2,1)S(1)} %copy-done), kind=kOutput, calls=%fused_computation.7 | convolution fusion | flops 3222798336 | bytes 10485760 | tf_op jit(solution)/shard_map/td,pdc->ptc/dot_general | solution.py:52
  104.9 1.2 fusion.14
  106.1 0.0 copy-start.1
  106.1 1.1 copy-done.1
  107.1 1.2 convolution_convert_fusion.1
  108.3 0.0 all-gather.9.cloned.1.call-update
  108.3 0.0 all-gather.7.cloned.1.call-start
  108.4 0.7 all-gather.7.cloned.1.call-update
  109.1 0.1 iota_compare_fusion
  109.2 1.6 copy.16
  110.8 5.1 %fusion = f32[8,512,128]{1,2,0:T(8,128)} fusion(bf16[8,512,128]{1,2,0:T(8,128)(2,1)S(1)} %bitcast.50, pred[512,512]{1,0:T(8,128)(4,1)S(1)} %iota_compare_fusion, bf16[8,512,128]{1,2,0:T(8,128)(2,1)} %bitcast.52, bf16[512,8,128]{2,0,1:T(8,128)(2,1)S(1)} %copy.16), kind=kOutput, calls=%fused_computation.2 | convolution fusion | flops 1077936128 | bytes 5505024 | tf_op jit(solution)/shard_map/hij,hje->hie/dot_general | solution.py:28
  115.9 43.0 %all-gather.9.cloned.1.call-done = bf16[128,128,128]{2,1,0:T(8,128)(2,1)} async-done(((bf16[8,128,128]{2,1,0:T(8,128)(2,1)}), bf16[128,128,128]{2,1,0:T(8,128)(2,1)}) %all-gather.9.cloned.1.call-update) | async-done | bytes 4194320 | tf_op jit(solution)/shard_map/all_gather | solution.py:12
  159.0 0.0 copy-start.2
  159.0 2.1 %multiply_reduce_fusion = (f32[8,512]{1,0:T(8,128)S(1)}, f32[8,512,128]{1,2,0:T(8,128)S(1)}) fusion(f32[8,512,128]{1,2,0:T(8,128)} %fusion, f32[8,128,128]{2,1,0:T(8,128)S(1)} %get-tuple-element.28, bf16[512,8,128]{2,0,1:T(8,128)(2,1)S(1)} %copy.16), kind=kOutput, calls=%fused_computation.11 | convolution fusion | flops 135917568 | bytes 5783552 | tf_op jit(solution)/shard_map/htd,hde->hte/dot_general | solution.py:42
  161.1 0.0 copy-done.2
  161.1 0.3 fusion.6
  161.4 30.7 %all-gather.7.cloned.1.call-done = bf16[1024,1024]{1,0:T(8,128)(2,1)} async-done(((bf16[512,1024]{1,0:T(8,128)(2,1)}), bf16[1024,1024]{1,0:T(8,128)(2,1)}) %all-gather.7.cloned.1.call-update) | async-done | bytes 2097168 | tf_op jit(solution)/shard_map/all_gather | solution.py:72
  192.1 3.8 %fusion.7 = bf16[1,512,1024]{2,1,0:T(8,128)(2,1)} fusion(bf16[512,1024]{0,1:T(8,128)(2,1)S(1)} %bitcast.54, bf16[1024,1024]{1,0:T(8,128)(2,1)} %all-gather.7.cloned.1.call-done), kind=kOutput, calls=%fused_computation.14 | convolution fusion | flops 1074266112 | bytes 4194304 | tf_op jit(solution)/shard_map/dot_general | solution.py:71
  (3 shorter events, 0.1 us)
Async XLA Ops:
  6.5 91.9 %copy-start = (bf16[1,512,1024]{2,1,0:T(8,128)(2,1)S(1)}, bf16[1,512,1024]{2,1,0:T(8,128)(2,1)}, u32[]{:S(2)}) copy-start(bf16[1,512,1024]{2,1,0:T(8,128)(2,1)} %param.8) | copy-start | bytes 3145732
  6.5 91.9 %all-gather.5.cloned.1.call-start = ((), (), s32[]{:S(2)}) async-start(), calls=%async_computation | async-start | bytes 9437184 | tf_op jit(solution)/shard_map/all_gather | solution.py:55
  15.2 143.7 %all-gather.9.cloned.1.call-start = ((), (), s32[]{:S(2)}) async-start(), calls=%async_computation.2 | async-start | bytes 4456448 | tf_op jit(solution)/shard_map/all_gather | solution.py:12
  106.1 1.1 copy-start.1
  108.3 83.8 %all-gather.7.cloned.1.call-start = ((), (), s32[]{:S(2)}) async-start(), calls=%async_computation.1 | async-start | bytes 3145728 | tf_op jit(solution)/shard_map/all_gather | solution.py:72
  159.0 2.1 %copy-start.2 = (f32[1024]{0:T(1024)S(1)}, f32[1024]{0:T(1024)}, u32[]{:S(2)}) copy-start(f32[1024]{0:T(1024)} %param.13) | copy-start | bytes 12292
Sparse Core Ops, SparseCore 0:
  15.3 83.0 all-gather.4
  108.5 50.3 all-gather.8
  160.5 31.6 all-gather.6
where the time goes:
time: 203 us; the launch traced here: 202 us
  waiting for transfers between devices  158 us (78%)
  matrix products  18.7 us (9%)
  between operations  13.2 us (7%)
  local copies, waits for them, and re-layouts  9.22 us (5%)
  other arithmetic  3.68 us (2%)
    all_gather x1, waiting for transfers between devices, body(): lax.all_gather(stacked, 'dp', axis=2, tiled=True)  83.2 us
    all_gather x1, waiting for transfers between devices, entering(): gathered = lax.all_gather(value.astype(jnp.bfloat16), axis)  43 us
    all_gather x1, waiting for transfers between devices, body(): lax.all_gather(w_out, 'dp', axis=0, tiled=True)  30.7 us
    dot_general x1, matrix products, body(): jnp.einsum('td,pdc->ptc', rows, lax.all_gather(stacked, 'dp', axis=2, til...  6.49 us
    unnamed x9, local copies, waits for them, and re-layouts  6.4 us
    dot_general x1, matrix products, inner_block(): jnp.einsum('hij,hje->hie', scores, value_heads, preferred_element_type=jn...  5.12 us
  transfers between devices with their start and end apart: 3, of which 3 were waited for; matrix products, arithmetic and copies ran while one was open for 5% of the time, Pallas kernels for 0%

commit v1 on v0

--- a/solution.py
+++ b/solution.py
@@ -5,6 +5,21 @@
 
 H = 8
 DH = 128
+
+
+def on_each_block(value, axis, dim, make, out_dim):
+    ways, here, step = (lax.axis_size(axis), lax.axis_index(axis), value.shape[dim])
+    results = []
+    for far in range(ways):
+        arriving = (
+            lax.ppermute(value, axis, [(d, (d + 1) % ways) for d in range(ways)])
+            if far + 1 < ways
+            else value
+        )
+        results.append(make(value, (here - far) % ways * step))
+        value = arriving
+    line = jnp.concatenate(results[::-1], axis=out_dim)
+    return jnp.roll(line, (here + 1) * results[0].shape[out_dim], axis=out_dim)
 
 
 def entering(value, axis, join, neutral):
@@ -49,11 +64,14 @@
     rows = tokens[0]
     length = rows.shape[0]
     stacked = jnp.stack([w_query, w_key, w_value], axis=0)
-    projected = jnp.einsum(
-        "td,pdc->ptc",
-        rows,
-        lax.all_gather(stacked, "dp", axis=2, tiled=True),
-        preferred_element_type=jnp.float32,
+    projected = on_each_block(
+        stacked,
+        "dp",
+        2,
+        lambda own_block, at: jnp.einsum(
+            "td,pdc->ptc", rows, own_block, preferred_element_type=jnp.float32
+        ),
+        2,
     ).astype(jnp.bfloat16)
     query = projected[0]
     key = projected[1]

time: 203 us -> 196 us (0.966)
  waiting for transfers between devices: 158 us -> 141 us
  other arithmetic: 3.68 us -> 9.54 us
  starting transfers between devices: 0.09 us -> 3.04 us
    all_gather x1 -> x0, waiting for transfers between devices: 83.2 us -> none  [body(): lax.all_gather(stacked, 'dp', axis=2, tiled=True)]
    ppermute x0 -> x1, waiting for transfers between devices: none -> 65.3 us  [on_each_block(): lax.ppermute(value, axis, [(d, (d + 1) % ways) for d in range(ways)])]
    convert_element_type x0 -> x1, other arithmetic: none -> 5.94 us  [body(): projected = on_each_block(stacked, 'dp', 2, lambda own_block, at: jnp.ein...]
    ppermute x0 -> x1, starting transfers between devices: none -> 3 us  [on_each_block(): lax.ppermute(value, axis, [(d, (d + 1) % ways) for d in range(ways)])]
    dot_general x1 -> x2, matrix products: 6.49 us -> 6.78 us  [body(): jnp.einsum('td,pdc->ptc', rows, own_block, preferred_element_type=jnp.flo...]
  transfers between devices with their start and end apart: 3 -> 3, of which waited for: 3 -> 3; matrix products, arithmetic and copies ran while one was open for 5% -> 6% of each run, Pallas kernels for 0% -> 0%
where the time goes in v1:
time: 196 us; the launch traced here: 195 us
  waiting for transfers between devices  141 us (72%)
  matrix products  19 us (10%)
  between operations  13.5 us (7%)
  other arithmetic  9.54 us (5%)
  local copies, waits for them, and re-layouts  9.23 us (5%)
  starting transfers between devices  3.04 us (2%)
    ppermute x1, waiting for transfers between devices, on_each_block(): lax.ppermute(value, axis, [(d, (d + 1) % ways) for d in range(ways)])  65.3 us
    all_gather x1, waiting for transfers between devices, entering(): gathered = lax.all_gather(value.astype(jnp.bfloat16), axis)  44.4 us
    all_gather x1, waiting for transfers between devices, body(): lax.all_gather(w_out, 'dp', axis=0, tiled=True)  30.7 us
    dot_general x2, matrix products, body(): jnp.einsum('td,pdc->ptc', rows, own_block, preferred_element_type=jnp.flo...  6.78 us
    unnamed x9, local copies, waits for them, and re-layouts  6.41 us
    convert_element_type x1, other arithmetic, body(): projected = on_each_block(stacked, 'dp', 2, lambda own_block, at: jnp.ein...  5.94 us
    dot_general x1, matrix products, inner_block(): jnp.einsum('hij,hje->hie', scores, value_heads, preferred_element_type=jn...  5.13 us
  transfers between devices with their start and end apart: 3, of which 3 were waited for; matrix products, arithmetic and copies ran while one was open for 6% of the time, Pallas kernels for 0%

profile of v1, /device:TPU:0, one launch (start us, length us, event | category | flops | bytes accessed | tf_op | source)
XLA Modules:
  0.0 195.5 jit_solution(4400005106560650813)
XLA Ops:
  6.5 0.0 copy-start
  6.5 0.0 all-gather.6.cloned.1.call-start
  6.5 1.6 copy.13
  8.1 1.5 copy.14
  9.6 2.3 %copy.15 = bf16[1024,512]{0,1:T(8,128)(2,1)} copy(bf16[1024,512]{1,0:T(8,128)(2,1)} %param.11) | data formatting | bytes 2097152 | tf_op args[3]
  11.9 3.2 %pad_maximum_fusion = bf16[3,1024,512]{1,2,0:T(8,128)(2,1)} fusion(bf16[1,1024,512]{1,2,0:T(8,128)(2,1)} %bitcast.57, bf16[1,1024,512]{1,2,0:T(8,128)(2,1)S(1)} %bitcast.55, bf16[1,1024,512]{1,2,0:T(8,128)(2,1)S(1)} %bitcast.53), kind=kLoop, calls=%fused_computation.14 | loop fusion | flops 3145728 | bytes 6291456 | tf_op jit(solution)/shard_map/stack | solution.py:66
  15.1 3.0 %collective-permute-start = (bf16[3,1024,512]{1,2,0:T(8,128)(2,1)}, bf16[3,1024,512]{1,2,0:T(8,128)(2,1)}, u32[]{:S(2)}, u32[]{:S(2)}) collective-permute-start(bf16[3,1024,512]{1,2,0:T(8,128)(2,1)} %pad_maximum_fusion), channel_id=1, source_target_pairs={{0,16},{16,0},{1,17},{17,1},{2,18},{18,2},{3,19},{19,3},{4,20},{20... | collective-permute-start | bytes 9437192 | tf_op jit(solution)/shard_map/ppermute | solution.py:15
  18.1 0.0 copy-done
  18.1 3.1 %convolution_bitcast_fusion = bf16[3,512,512]{1,2,0:T(8,128)(2,1)S(1)} fusion(bf16[1,512,1024]{2,1,0:T(8,128)(2,1)S(1)} %copy-done, bf16[1,1024,512]{1,2,0:T(8,128)(2,1)} %bitcast.58, bf16[1,1024,512]{1,2,0:T(8,128)(2,1)S(1)} %bitcast.56, bf16[1,1024,512]{1,2,0:T(8,128)(2,1)S(1)} %bitcast.54), kind=kOutput, calls=%fused_computation.19 | convolution fusion | flops 1613758464 | bytes 5767168 | tf_op jit(solution)/shard_map/td,pdc->ptc/dot_general | solution.py:71
  21.1 65.3 %collective-permute-done = bf16[3,1024,512]{1,2,0:T(8,128)(2,1)} collective-permute-done((bf16[3,1024,512]{1,2,0:T(8,128)(2,1)}, bf16[3,1024,512]{1,2,0:T(8,128)(2,1)}, u32[]{:S(2)}, u32[]{:S(2)}) %collective-permute-start) | collective-permute-done | bytes 3145760 | tf_op jit(solution)/shard_map/ppermute | solution.py:15
  86.5 3.7 %convolution_bitcast_fusion.1 = bf16[3,512,512]{1,2,0:T(8,128)(2,1)S(1)} fusion(bf16[3,1024,512]{1,2,0:T(8,128)(2,1)} %collective-permute-done, bf16[1,512,1024]{2,1,0:T(8,128)(2,1)S(1)} %copy-done), kind=kOutput, calls=%fused_computation.20 | convolution fusion | flops 1610612736 | bytes 5767168 | tf_op jit(solution)/shard_map/td,pdc->ptc/dot_general | solution.py:71
  90.2 5.9 %fusion.3 = bf16[3,512,1024]{1,2,0:T(8,128)(2,1)S(1)} fusion(s32[]{:T(128)S(6)} %select_n.22, bf16[3,512,512]{1,2,0:T(8,128)(2,1)S(1)} %convolution_bitcast_fusion.1, bf16[3,512,512]{1,2,0:T(8,128)(2,1)S(1)} %convolution_bitcast_fusion), kind=kLoop, calls=%fused_computation.9 | loop fusion | flops 12582912 | bytes 6291460 | tf_op jit(solution)/shard_map/convert_element_type | solution.py:75
  96.2 1.2 fusion.19
  97.3 0.0 copy-start.1
  97.3 1.1 copy-done.1
  98.4 1.2 convolution_convert_fusion.1
  99.6 0.0 all-gather.6.cloned.1.call-update
  99.6 0.0 all-gather.4.cloned.1.call-start
  99.6 0.7 all-gather.4.cloned.1.call-update
  100.4 0.1 iota_compare_fusion
  100.4 1.6 copy.16
  102.1 5.1 %fusion.4 = f32[8,512,128]{1,2,0:T(8,128)} fusion(bf16[8,512,128]{1,2,0:T(8,128)(2,1)S(1)} %bitcast.60, pred[512,512]{1,0:T(8,128)(4,1)S(1)} %iota_compare_fusion, bf16[8,512,128]{1,2,0:T(8,128)(2,1)} %bitcast.62, bf16[512,8,128]{2,0,1:T(8,128)(2,1)S(1)} %copy.16), kind=kOutput, calls=%fused_computation.10 | convolution fusion | flops 1077936128 | bytes 5505024 | tf_op jit(solution)/shard_map/hij,hje->hie/dot_general | solution.py:43
  107.2 44.4 %all-gather.6.cloned.1.call-done = bf16[128,128,128]{2,1,0:T(8,128)(2,1)} async-done(((bf16[8,128,128]{2,1,0:T(8,128)(2,1)}), bf16[128,128,128]{2,1,0:T(8,128)(2,1)}) %all-gather.6.cloned.1.call-update) | async-done | bytes 4194320 | tf_op jit(solution)/shard_map/all_gather | solution.py:27
  151.7 0.0 copy-start.2
  151.7 2.1 %multiply_reduce_fusion = (f32[8,512]{1,0:T(8,128)S(1)}, f32[8,512,128]{1,2,0:T(8,128)S(1)}) fusion(f32[8,512,128]{1,2,0:T(8,128)} %fusion.4, f32[8,128,128]{2,1,0:T(8,128)S(1)} %get-tuple-element.28, bf16[512,8,128]{2,0,1:T(8,128)(2,1)S(1)} %copy.16), kind=kOutput, calls=%fused_computation.18 | convolution fusion | flops 135917568 | bytes 5783552 | tf_op jit(solution)/shard_map/htd,hde->hte/dot_general | solution.py:57
  153.8 0.0 copy-done.2
  153.8 0.3 fusion.10
  154.1 30.7 %all-gather.4.cloned.1.call-done = bf16[1024,1024]{1,0:T(8,128)(2,1)} async-done(((bf16[512,1024]{1,0:T(8,128)(2,1)}), bf16[1024,1024]{1,0:T(8,128)(2,1)}) %all-gather.4.cloned.1.call-update) | async-done | bytes 2097168 | tf_op jit(solution)/shard_map/all_gather | solution.py:90
  184.8 3.8 %fusion.11 = bf16[1,512,1024]{2,1,0:T(8,128)(2,1)} fusion(bf16[512,1024]{0,1:T(8,128)(2,1)S(1)} %bitcast.64, bf16[1024,1024]{1,0:T(8,128)(2,1)} %all-gather.4.cloned.1.call-done), kind=kOutput, calls=%fused_computation.23 | convolution fusion | flops 1074266112 | bytes 4194304 | tf_op jit(solution)/shard_map/dot_general | solution.py:89
  (3 shorter events, 0.1 us)
Async XLA Ops:
  6.5 11.5 %copy-start = (bf16[1,512,1024]{2,1,0:T(8,128)(2,1)S(1)}, bf16[1,512,1024]{2,1,0:T(8,128)(2,1)}, u32[]{:S(2)}) copy-start(bf16[1,512,1024]{2,1,0:T(8,128)(2,1)} %param.8) | copy-start | bytes 3145732
  6.5 145.1 %all-gather.6.cloned.1.call-start = ((), (), s32[]{:S(2)}) async-start(), calls=%async_computation.1 | async-start | bytes 4456448 | tf_op jit(solution)/shard_map/all_gather | solution.py:27
  15.1 71.4 %collective-permute-start = (bf16[3,1024,512]{1,2,0:T(8,128)(2,1)}, bf16[3,1024,512]{1,2,0:T(8,128)(2,1)}, u32[]{:S(2)}, u32[]{:S(2)}) collective-permute-start(bf16[3,1024,512]{1,2,0:T(8,128)(2,1)} %pad_maximum_fusion), channel_id=1, source_target_pairs={{0,16},{16,0},{1,17},{17,1},{2,18},{18,2},{3,19},{19,3},{4,20},{20... | collective-permute-start | bytes 9437192 | tf_op jit(solution)/shard_map/ppermute | solution.py:15
  97.3 1.1 copy-start.1
  99.6 85.2 %all-gather.4.cloned.1.call-start = ((), (), s32[]{:S(2)}) async-start(), calls=%async_computation | async-start | bytes 3145728 | tf_op jit(solution)/shard_map/all_gather | solution.py:90
  151.7 2.1 %copy-start.2 = (f32[1024]{0:T(1024)S(1)}, f32[1024]{0:T(1024)}, u32[]{:S(2)}) copy-start(f32[1024]{0:T(1024)} %param.13) | copy-start | bytes 12292
Sparse Core Ops, SparseCore 0:
  99.7 51.8 all-gather.5
  153.1 31.6 all-gather.3
